TPU v7x, 32 devices: a whole 2x2x4 slice. The times are simulated.
32 devices in a mesh: grp: 2 (over y), blk: 4 (over z), sub: 2 (over x), pair: 2 (over core).
Axes of the slice: x: 2, y: 2, z: 4, core: 2. Of those that a mesh axis runs over, the one named last changes fastest.
Arguments:
- grad_volume: bfloat16 [16, 128, 8192], P(('grp', 'blk', 'sub'), 'pair'), parts along dimension 0, may hold values from -6 to 6
- query_feats: bfloat16 [16384, 1024], P(('grp', 'blk')), parts along dimension 0, may hold values from -6 to 6
- support_feats: bfloat16 [16, 128, 1024], P(('grp', 'blk', 'sub'), 'pair'), parts along dimension 0, may hold values from -6 to 6
- query_kernel: float32 [3, 3], replicated, may hold values from -2 to 2
- support_kernel: float32 [3, 3], replicated, may hold values from -2 to 2
Outputs:
- query_grad: float32 [16384, 1024], P(('grp', 'blk', 'sub', 'pair')), parts along dimension 0
- support_grad: float32 [16, 128, 1024], P(('grp', 'blk', 'sub'), 'pair'), parts along dimension 0
There are 2 independent parts, one for each index of `grp`. A program takes and returns all parts, laid end to end along the dimension named above; an argument that names none is the same for every part. Nothing has to cross between parts.
All inputs are finite; a program needn't handle non-finite values.
Results may differ from a plain program's by a relative error of at most 0.0029.
Values may be sent and summed in bfloat16 or wider, within the bound.
No kernel may reach another device: no remote copies, remote signals or barrier semaphores. Data moves between devices by JAX's collectives and lax.ppermute only.
A program may use at most 64 MiB of HBM per device.

v0:
```python
import math
import jax
import jax.numpy as jnp
from jax import lax
from jax.sharding import PartitionSpec as P

QW = 128
QH = 64


def extended(cells, sides, width):
    for axis, dim in sides:
        count = lax.axis_size(axis)
        ends = count - 1
        head = lax.slice_in_dim(cells, 0, width, axis=dim)
        tail = lax.slice_in_dim(cells, cells.shape[dim] - width, cells.shape[dim], axis=dim)
        cells = jnp.concatenate(
            [
                lax.ppermute(tail, axis, [(i, (i + 1) % count) for i in range(ends)]),
                cells,
                lax.ppermute(head, axis, [((i + 1) % count, i) for i in range(ends)]),
            ],
            axis=dim,
        )
    return cells


def shifted(value, axis, steps):
    count = lax.axis_size(axis)
    pairs = [(source, (source + steps) % count) for source in range(count)]
    return lax.ppermute(value, axis, pairs)


def query_pass(volume, kernel):
    planes, columns, queries = volume.shape
    grid = volume.astype(jnp.float32).reshape(planes, columns, QH, QW)
    padded = jnp.pad(grid, ((0, 0), (0, 0), (1, 1), (1, 1)))
    total = jnp.zeros_like(grid)
    for row_shift in range(3):
        for col_shift in range(3):
            total = (
                total
                + kernel[row_shift, col_shift]
                * padded[:, :, row_shift : row_shift + QH, col_shift : col_shift + QW]
            )
    return total.reshape(planes, columns, queries)


def support_pass(rimmed, kernel, planes, columns):
    total = jnp.zeros((planes, columns, rimmed.shape[2]), jnp.float32)
    for row_shift in range(3):
        for col_shift in range(3):
            total = total + kernel[row_shift, col_shift] * rimmed[
                row_shift : row_shift + planes, col_shift : col_shift + columns
            ].astype(jnp.float32)
    return total


def shards(grad_volume, query_feats, support_feats, query_kernel, support_kernel):
    planes, columns, queries = grad_volume.shape
    rimmed = extended(grad_volume, ((("blk", "sub"), 0), ("pair", 1)), 1)
    corr_grad = (
        query_pass(grad_volume, query_kernel)
        + support_pass(rimmed, support_kernel, planes, columns)
    ).astype(jnp.bfloat16)
    moved = lax.all_to_all(corr_grad, "blk", split_axis=2, concat_axis=0, tiled=True)
    cycle_size = lax.axis_size("blk")
    own_index = lax.axis_index("blk")
    tile_len = moved.shape[2]
    tiles = moved.reshape(cycle_size, planes, columns, tile_len)
    width = query_feats.shape[1]
    scale_factor = 1.0 / math.sqrt(width)

    def project(piece_index, feat_piece, acc_piece, count):
        whole_block = lax.dynamic_index_in_dim(tiles, piece_index, 0, keepdims=False)
        block = whole_block.reshape(planes * count, tile_len)
        feat_flat = feat_piece.reshape(planes * count, width)
        query_term = lax.dot_general(
            block, feat_flat, (((0,), (0,)), ((), ())), preferred_element_type=jnp.float32
        )
        acc_new = acc_piece + jnp.dot(
            block, query_feats, preferred_element_type=jnp.float32
        ).reshape(planes, count, width)
        return (query_term, acc_new)

    query_start = jnp.zeros((tile_len, width), jnp.float32)

    def turn_one(turn_index, carry):
        query_total, feat_piece, acc_piece = carry
        term_piece, acc_piece = project(
            (own_index - turn_index) % cycle_size, feat_piece, acc_piece, columns
        )
        feat_piece = shifted(feat_piece, "blk", 1)
        acc_piece = shifted(acc_piece, "blk", 1)
        return (query_total + term_piece, feat_piece, acc_piece)

    start = (query_start, support_feats, jnp.zeros((planes, columns, width), jnp.float32))
    query_total, feat_piece, support_total = lax.fori_loop(0, cycle_size, turn_one, start)
    query_grad = (
        lax.psum_scatter(query_total, ("sub", "pair"), scatter_dimension=0, tiled=True)
        * scale_factor
    )
    return (query_grad, support_total * scale_factor)


def solution(mesh):
    in_specs = (
        P(("grp", "blk", "sub"), "pair", None),
        P(("grp", "blk"), None),
        P(("grp", "blk", "sub"), "pair", None),
        P(),
        P(),
    )
    out_specs = (P(("grp", "blk", "sub", "pair"), None), P(("grp", "blk", "sub"), "pair", None))
    return jax.shard_map(shards, mesh=mesh, in_specs=in_specs, out_specs=out_specs, check_vma=False)
```

profile of v0, /device:TPU:0, one launch (start us, length us, event | category | flops | bytes accessed | tf_op | source)
XLA Modules:
  0.0 318.6 jit_solution(11927447084421412007)
XLA Ops:
  7.2 5.0 %collective-permute-start.2 = (bf16[1,64,8192]{2,1,0:T(8,128)(2,1)}, bf16[1,64,8192]{2,1,0:T(8,128)(2,1)S(1)}, u32[]{:S(2)}, u32[]{:S(2)}) collective-permute-start(bf16[1,64,8192]{2,1,0:T(8,128)(2,1)} %param.7), channel_id=1, source_target_pairs={{0,2},{2,4},{4,6},{6,8},{8,10},{10,12},{12,14},{1,3},{3,5},{5,7},{... | collective-permute-start | bytes 3145736 | tf_op jit(solution)/shard_map/ppermute | solution.py:19
  12.2 1.3 collective-permute-start.3
  13.5 1.7 fusion.33
  15.2 1.7 fusion.32
  16.9 40.4 %collective-permute-done.2 = bf16[1,64,8192]{2,1,0:T(8,128)(2,1)S(1)} collective-permute-done((bf16[1,64,8192]{2,1,0:T(8,128)(2,1)}, bf16[1,64,8192]{2,1,0:T(8,128)(2,1)S(1)}, u32[]{:S(2)}, u32[]{:S(2)}) %collective-permute-start.2) | collective-permute-done | bytes 1048608 | tf_op jit(solution)/shard_map/ppermute | solution.py:19
  57.4 0.2 constant_dynamic-update-slice_fusion.1
  57.7 0.1 constant_dynamic-update-slice_fusion
  57.8 0.2 fusion.31
  57.9 0.1 copy.21
  58.0 0.1 copy.22
  58.1 1.3 collective-permute-start.5
  59.4 3.0 collective-permute-start.4
  62.4 0.4 copy.23
  62.8 9.4 %fusion.23 = f32[1,64,64,128]{3,2,1,0:T(8,128)S(1)} fusion(f32[1,64,64,128]{3,2,1,0:T(8,128)S(1)} %bitcast.53, f32[]{:T(128)} %bitcast.8, f32[]{:T(128)} %bitcast.7, f32[]{:T(128)} %bitcast.6, f32[]{:T(128)} %bitcast.5, f32[]{:T(128)} %bitcast.4, f32[]{:T(128)} %bitcast.3, f32[]{:T(128)} %bitcast.2, f32[]{:T(128)} %bitcast.1, f32[]{:T(128)} %bitcast), kind=kLoop, calls=%fused_computation.35 | loop fusion | flops 8912896 | bytes 4194340 | tf_op jit(solution)/shard_map/add | solution.py:42
  72.3 1.5 reshape.56
  73.8 0.1 copy.17
  73.9 0.1 copy.15
  74.0 11.4 %fusion.14 = bf16[1,64,8192]{2,1,0:T(8,128)(2,1)S(1)} fusion(f32[1,64,8192]{2,1,0:T(8,128)} %reshape.56, bf16[1,64,8192]{2,1,0:T(8,128)(2,1)} %param.7, bf16[1,64,8192]{2,1,0:T(8,128)(2,1)} %copy-done.2, bf16[1,64,8192]{2,1,0:T(8,128)(2,1)S(1)} %collective-permute-done.2, bf16[3,1,8192]{2,1,0:T(2,128)(2,1)S(1)} %copy.17, bf16[3,64,8192]{2,1,0:T(8,128)(2,1)} %copy-done, ...), kind=kLoop, calls=%fused_computation.26 | loop fusion | flops 24117248 | bytes 9535524 | tf_op jit(solution)/shard_map/convert_element_type | solution.py:65
  85.4 6.8 %copy.18 = bf16[1,64,8192]{1,0,2:T(2,128)(2,1)} copy(bf16[1,64,8192]{2,1,0:T(8,128)(2,1)S(1)} %fusion.14) | data formatting | bytes 2097152 | tf_op jit(solution)/shard_map/convert_element_type | solution.py:65
  92.2 0.5 broadcast.17
  92.7 45.2 %reduce = bf16[8192,64]{1,0:T(8,128)(2,1)S(1)} reduce(bf16[8192,1,64]{2,1,0:T(2,128)(2,1)} %bitcast.51, bf16[]{:T(256)} %broadcast.17), dimensions={1}, to_apply=%bitcast.38.reduce_sub_computation | reduce | bytes 2097154
  138.0 2.7 reshape.60
  140.6 6.3 %all-to-all-start = ((bf16[4,2,65536]{2,1,0:T(2,128)(2,1)}), bf16[4,2,65536]{2,1,0:T(2,128)(2,1)S(1)}, u32[]{:S(2)}, u32[]{:S(2)}) async-start(bf16[4,2,65536]{2,1,0:T(2,128)(2,1)} %reshape.60), calls=%async_computation | async-start | bytes 2097152 | tf_op jit(solution)/shard_map/all_to_all | solution.py:66
  146.9 25.3 %all-to-all-done = bf16[4,2,65536]{2,1,0:T(2,128)(2,1)S(1)} async-done(((bf16[4,2,65536]{2,1,0:T(2,128)(2,1)}), bf16[4,2,65536]{2,1,0:T(2,128)(2,1)S(1)}, u32[]{:S(2)}, u32[]{:S(2)}) %all-to-all-start) | async-done | bytes 1048608 | tf_op jit(solution)/shard_map/all_to_all | solution.py:66
  172.2 3.2 reshape.61
  175.4 8.2 %copy.19 = bf16[1,64,8192]{2,1,0:T(8,128)(2,1)S(1)} copy(bf16[1,64,8192]{1,0,2:T(2,128)(2,1)} %bitcast.52) | data formatting | bytes 2097152 | tf_op jit(solution)/shard_map/all_to_all | solution.py:66
  183.5 0.8 all_to_all.12
  184.3 0.6 copy.20
  185.0 52.0 %while.20 = (s32[]{:T(128)}, f32[2048,1024]{1,0:T(8,128)}, bf16[1,64,1024]{2,1,0:T(8,128)(2,1)S(1)}, f32[1,64,1024]{2,1,0:T(8,128)S(1)}, s32[]{:T(128)}, /*index...) while((s32[]{:T(128)}, f32[2048,1024]{1,0:T(8,128)}, ...), condition=%wide.region_1.2_spmd.clone, body=%wide.region_0.1_spmd.clone.sunk | while | flops 541130752 | bytes 23986536 | solution.py:98
  185.1 3.0 fusion.44
  188.1 0.2 collective-permute-start.1
  188.4 4.5 %select_add_fusion.2 = f32[2048,1024]{1,0:T(8,128)} fusion(f32[2048,1024]{1,0:T(8,128)} %get-tuple-element.318, pred[]{:T(512)S(6)} %compare.5, bf16[4,1,64,2048]{3,2,1,0:T(8,128)(2,1)S(1)} %get-tuple-element.333, s32[]{:T(128)S(6)} %select_n.36, bf16[1,64,1024]{2,1,0:T(8,128)(2,1)S(1)} %copy.32), kind=kOutput, calls=%fused_computation.clone.1 | convolution fusion | flops 272629760 | bytes 17170436 | tf_op jit(solution)/shard_map/while/body/eval_jaxpr/dot_general | solution.py:78
  192.9 4.6 %collective-permute-done.1 = f32[1,64,1024]{2,1,0:T(8,128)S(1)} collective-permute-done((f32[1,64,1024]{2,1,0:T(8,128)S(1)}, f32[1,64,1024]{2,1,0:T(8,128)S(1)}, u32[]{:S(2)}, u32[]{:S(2)}) %collective-permute-start.1) | collective-permute-done | bytes 262176 | tf_op jit(solution)/shard_map/while/body/eval_jaxpr/ppermute | solution.py:31
  197.5 3.0 fusion.44
  200.6 0.2 collective-permute-start.1
  200.8 7.9 %select_add_fusion.2 = f32[2048,1024]{1,0:T(8,128)} fusion(f32[2048,1024]{1,0:T(8,128)} %get-tuple-element.318, pred[]{:T(512)S(6)} %compare.5, bf16[4,1,64,2048]{3,2,1,0:T(8,128)(2,1)S(1)} %get-tuple-element.333, s32[]{:T(128)S(6)} %select_n.36, bf16[1,64,1024]{2,1,0:T(8,128)(2,1)S(1)} %copy.32), kind=kOutput, calls=%fused_computation.clone.1 | convolution fusion | flops 272629760 | bytes 17170436 | tf_op jit(solution)/shard_map/while/body/eval_jaxpr/dot_general | solution.py:78
  208.6 1.2 collective-permute-done.1
  209.9 1.3 collective-permute-start
  211.2 3.0 fusion.44
  214.2 2.4 collective-permute-start.1
  216.6 7.9 %select_add_fusion.2 = f32[2048,1024]{1,0:T(8,128)} fusion(f32[2048,1024]{1,0:T(8,128)} %get-tuple-element.318, pred[]{:T(512)S(6)} %compare.5, bf16[4,1,64,2048]{3,2,1,0:T(8,128)(2,1)S(1)} %get-tuple-element.333, s32[]{:T(128)S(6)} %select_n.36, bf16[1,64,1024]{2,1,0:T(8,128)(2,1)S(1)} %copy.32), kind=kOutput, calls=%fused_computation.clone.1 | convolution fusion | flops 272629760 | bytes 17170436 | tf_op jit(solution)/shard_map/while/body/eval_jaxpr/dot_general | solution.py:78
  224.5 0.1 collective-permute-start
  224.6 3.0 fusion.44
  227.6 1.4 collective-permute-start.1
  229.0 7.9 %select_add_fusion.2 = f32[2048,1024]{1,0:T(8,128)} fusion(f32[2048,1024]{1,0:T(8,128)} %get-tuple-element.318, pred[]{:T(512)S(6)} %compare.5, bf16[4,1,64,2048]{3,2,1,0:T(8,128)(2,1)S(1)} %get-tuple-element.333, s32[]{:T(128)S(6)} %select_n.36, bf16[1,64,1024]{2,1,0:T(8,128)(2,1)S(1)} %copy.32), kind=kOutput, calls=%fused_computation.clone.1 | convolution fusion | flops 272629760 | bytes 17170436 | tf_op jit(solution)/shard_map/while/body/eval_jaxpr/dot_general | solution.py:78
  236.9 0.7 broadcast_multiply_fusion.1
  237.7 70.9 %reduce-scatter.2.cloned.1.call-done = f32[512,1024]{1,0:T(8,128)} async-done(((f32[2048,1024]{1,0:T(8,128)}), f32[512,1024]{1,0:T(8,128)}) %reduce-scatter.2.cloned.1.call-update) | async-done | bytes 2097168 | tf_op jit(solution)/shard_map/reduce_scatter | solution.py:100
  308.5 3.2 %broadcast_multiply_fusion = f32[512,1024]{1,0:T(8,128)} fusion(f32[512,1024]{1,0:T(8,128)} %reduce-scatter.2.cloned.1.call-done), kind=kLoop, calls=%fused_computation.45 | loop fusion | flops 524288 | bytes 4194304 | tf_op jit(solution)/shard_map/mul | solution.py:100
  (28 shorter events, 0.3 us)
Async XLA Ops:
  7.2 50.3 %copy-start.3 = (bf16[1,64,8192]{2,1,0:T(8,128)(2,1)S(1)}, bf16[1,64,8192]{2,1,0:T(8,128)(2,1)}, u32[]{:S(2)}) copy-start(bf16[1,64,8192]{2,1,0:T(8,128)(2,1)} %param.7) | copy-start | bytes 3145732
  7.2 50.2 %collective-permute-start.2 = (bf16[1,64,8192]{2,1,0:T(8,128)(2,1)}, bf16[1,64,8192]{2,1,0:T(8,128)(2,1)S(1)}, u32[]{:S(2)}, u32[]{:S(2)}) collective-permute-start(bf16[1,64,8192]{2,1,0:T(8,128)(2,1)} %param.7), channel_id=1, source_target_pairs={{0,2},{2,4},{4,6},{6,8},{8,10},{10,12},{12,14},{1,3},{3,5},{5,7},{... | collective-permute-start | bytes 3145736 | tf_op jit(solution)/shard_map/ppermute | solution.py:19
  12.2 45.5 %collective-permute-start.3 = (bf16[1,64,8192]{2,1,0:T(8,128)(2,1)}, bf16[1,64,8192]{2,1,0:T(8,128)(2,1)S(1)}, u32[]{:S(2)}, u32[]{:S(2)}) collective-permute-start(bf16[1,64,8192]{2,1,0:T(8,128)(2,1)} %param.7), channel_id=1, source_target_pairs={{2,0},{4,2},{6,4},{8,6},{10,8},{12,10},{14,12},{3,1},{5,3},{7,5},{... | collective-permute-start | bytes 3145736 | tf_op jit(solution)/shard_map/ppermute | solution.py:21
  57.7 5.1 %copy-start.2 = (bf16[1,64,8192]{2,1,0:T(8,128)(2,1)}, bf16[1,64,8192]{2,1,0:T(8,128)(2,1)S(1)}, u32[]{:S(2)}) copy-start(bf16[1,64,8192]{2,1,0:T(8,128)(2,1)S(1)} %collective-permute-done.3) | copy-start | bytes 3145732
  57.8 5.1 %copy-start = (bf16[3,64,8192]{2,1,0:T(8,128)(2,1)}, bf16[3,64,8192]{2,1,0:T(8,128)(2,1)S(1)}, u32[]{:S(2)}) copy-start(bf16[3,64,8192]{2,1,0:T(8,128)(2,1)S(1)} %constant_dynamic-update-slice_fusion) | copy-start | bytes 9437188
  58.1 15.7 %collective-permute-start.5 = (bf16[3,1,8192]{2,0,1:T(4,128)(2,1)S(1)}, bf16[3,1,8192]{2,0,1:T(4,128)(2,1)S(1)}, u32[]{:S(2)}, u32[]{:S(2)}) collective-permute-start(bf16[3,1,8192]{2,0,1:T(4,128)(2,1)S(1)} %copy.22), channel_id=1, source_target_pairs={{1,0},{3,2},{5,4},{7,6},{9,8},{11,10},{13,12},{15,14},{17,16},{19,... | collective-permute-start | bytes 147464 | tf_op jit(solution)/shard_map/ppermute | solution.py:21
  59.4 14.5 %collective-permute-start.4 = (bf16[3,1,8192]{2,0,1:T(4,128)(2,1)S(1)}, bf16[3,1,8192]{2,0,1:T(4,128)(2,1)S(1)}, u32[]{:S(2)}, u32[]{:S(2)}) collective-permute-start(bf16[3,1,8192]{2,0,1:T(4,128)(2,1)S(1)} %copy.21), channel_id=1, source_target_pairs={{0,1},{2,3},{4,5},{6,7},{8,9},{10,11},{12,13},{14,15},{16,17},{18,... | collective-permute-start | bytes 147464 | tf_op jit(solution)/shard_map/ppermute | solution.py:19
  140.6 31.6 %all-to-all-start = ((bf16[4,2,65536]{2,1,0:T(2,128)(2,1)}), bf16[4,2,65536]{2,1,0:T(2,128)(2,1)S(1)}, u32[]{:S(2)}, u32[]{:S(2)}) async-start(bf16[4,2,65536]{2,1,0:T(2,128)(2,1)} %reshape.60), calls=%async_computation | async-start | bytes 2097152 | tf_op jit(solution)/shard_map/all_to_all | solution.py:66
  146.9 161.6 %reduce-scatter.2.cloned.1.call-start = ((), (), s32[]{:S(2)}) async-start(), calls=%async_computation.2 | async-start | bytes 10485760 | tf_op jit(solution)/shard_map/reduce_scatter | solution.py:100
  183.5 1.4 copy-start.1
  185.0 7.9 %collective-permute-start = (bf16[1,64,1024]{2,1,0:T(8,128)(2,1)S(1)}, bf16[1,64,1024]{2,1,0:T(8,128)(2,1)S(1)}, u32[]{:S(2)}, u32[]{:S(2)}) collective-permute-start(bf16[1,64,1024]{2,1,0:T(8,128)(2,1)S(1)} %copy.32), channel_id=1, source_target_pairs={{0,4},{4,8},{8,12},{12,0},{1,5},{5,9},{9,13},{13,1},{2,6},{6,10},{... | collective-permute-start | bytes 393224 | tf_op jit(solution)/shard_map/while/body/eval_jaxpr/ppermute | solution.py:31
  188.1 9.3 %collective-permute-start.1 = (f32[1,64,1024]{2,1,0:T(8,128)S(1)}, f32[1,64,1024]{2,1,0:T(8,128)S(1)}, u32[]{:S(2)}, u32[]{:S(2)}) collective-permute-start(f32[1,64,1024]{2,1,0:T(8,128)S(1)} %fusion.44), channel_id=1, source_target_pairs={{0,4},{4,8},{8,12},{12,0},{1,5},{5,9},{9,13},{13,1},{2,6},{6,10},{... | collective-permute-start | bytes 786440 | tf_op jit(solution)/shard_map/while/body/eval_jaxpr/ppermute | solution.py:31
  197.4 11.2 %collective-permute-start = (bf16[1,64,1024]{2,1,0:T(8,128)(2,1)S(1)}, bf16[1,64,1024]{2,1,0:T(8,128)(2,1)S(1)}, u32[]{:S(2)}, u32[]{:S(2)}) collective-permute-start(bf16[1,64,1024]{2,1,0:T(8,128)(2,1)S(1)} %copy.32), channel_id=1, source_target_pairs={{0,4},{4,8},{8,12},{12,0},{1,5},{5,9},{9,13},{13,1},{2,6},{6,10},{... | collective-permute-start | bytes 393224 | tf_op jit(solution)/shard_map/while/body/eval_jaxpr/ppermute | solution.py:31
  200.6 9.3 %collective-permute-start.1 = (f32[1,64,1024]{2,1,0:T(8,128)S(1)}, f32[1,64,1024]{2,1,0:T(8,128)S(1)}, u32[]{:S(2)}, u32[]{:S(2)}) collective-permute-start(f32[1,64,1024]{2,1,0:T(8,128)S(1)} %fusion.44), channel_id=1, source_target_pairs={{0,4},{4,8},{8,12},{12,0},{1,5},{5,9},{9,13},{13,1},{2,6},{6,10},{... | collective-permute-start | bytes 786440 | tf_op jit(solution)/shard_map/while/body/eval_jaxpr/ppermute | solution.py:31
  209.9 14.6 %collective-permute-start = (bf16[1,64,1024]{2,1,0:T(8,128)(2,1)S(1)}, bf16[1,64,1024]{2,1,0:T(8,128)(2,1)S(1)}, u32[]{:S(2)}, u32[]{:S(2)}) collective-permute-start(bf16[1,64,1024]{2,1,0:T(8,128)(2,1)S(1)} %copy.32), channel_id=1, source_target_pairs={{0,4},{4,8},{8,12},{12,0},{1,5},{5,9},{9,13},{13,1},{2,6},{6,10},{... | collective-permute-start | bytes 393224 | tf_op jit(solution)/shard_map/while/body/eval_jaxpr/ppermute | solution.py:31
  214.2 10.3 %collective-permute-start.1 = (f32[1,64,1024]{2,1,0:T(8,128)S(1)}, f32[1,64,1024]{2,1,0:T(8,128)S(1)}, u32[]{:S(2)}, u32[]{:S(2)}) collective-permute-start(f32[1,64,1024]{2,1,0:T(8,128)S(1)} %fusion.44), channel_id=1, source_target_pairs={{0,4},{4,8},{8,12},{12,0},{1,5},{5,9},{9,13},{13,1},{2,6},{6,10},{... | collective-permute-start | bytes 786440 | tf_op jit(solution)/shard_map/while/body/eval_jaxpr/ppermute | solution.py:31
  224.5 12.4 %collective-permute-start = (bf16[1,64,1024]{2,1,0:T(8,128)(2,1)S(1)}, bf16[1,64,1024]{2,1,0:T(8,128)(2,1)S(1)}, u32[]{:S(2)}, u32[]{:S(2)}) collective-permute-start(bf16[1,64,1024]{2,1,0:T(8,128)(2,1)S(1)} %copy.32), channel_id=1, source_target_pairs={{0,4},{4,8},{8,12},{12,0},{1,5},{5,9},{9,13},{13,1},{2,6},{6,10},{... | collective-permute-start | bytes 393224 | tf_op jit(solution)/shard_map/while/body/eval_jaxpr/ppermute | solution.py:31
  227.6 9.3 %collective-permute-start.1 = (f32[1,64,1024]{2,1,0:T(8,128)S(1)}, f32[1,64,1024]{2,1,0:T(8,128)S(1)}, u32[]{:S(2)}, u32[]{:S(2)}) collective-permute-start(f32[1,64,1024]{2,1,0:T(8,128)S(1)} %fusion.44), channel_id=1, source_target_pairs={{0,4},{4,8},{8,12},{12,0},{1,5},{5,9},{9,13},{13,1},{2,6},{6,10},{... | collective-permute-start | bytes 786440 | tf_op jit(solution)/shard_map/while/body/eval_jaxpr/ppermute | solution.py:31
Sparse Core Ops, SparseCore 0:
  237.1 71.4 reduce-scatter.1
where the time goes:
time: 320 us; the launch traced here: 319 us
  waiting for transfers between devices  142 us (44%)
  other arithmetic  70.3 us (22%)
  matrix products  40.3 us (13%)
  local copies, waits for them, and re-layouts  28.6 us (9%)
  starting transfers between devices  22.6 us (7%)
  between operations  14.2 us (4%)
    reduce_scatter x1, waiting for transfers between devices, shards(): lax.psum_scatter(query_total, ('sub', 'pair'), scatter_dimension=0, tiled...  70.9 us
    unnamed x3, other arithmetic  45.5 us
    ppermute x2, waiting for transfers between devices, extended(): lax.ppermute(tail, axis, [(i, (i + 1) % count) for i in range(ends)])  40.4 us
    dot_general x4, matrix products, project(): lax.dot_general(block, feat_flat, (((0,), (0,)), ((), ())), preferred_ele...  28.1 us
    all_to_all x1, waiting for transfers between devices, shards(): lax.all_to_all(corr_grad, 'blk', split_axis=2, concat_axis=0, tiled=True)  25.3 us
    dot_general x4, matrix products, project(): jnp.dot(block, query_feats, preferred_element_type=jnp.float32)  12.1 us
    convert_element_type x1, other arithmetic, shards(): corr_grad = (query_pass(grad_volume, query_kernel) + support_pass(rimmed,...  11.4 us
    add x1, other arithmetic, query_pass(): total + kernel[row_shift, col_shift] * padded[:, :, row_shift:row_shift +...  9.43 us
  transfers between devices with their start and end apart: 14, of which 5 were waited for; matrix products, arithmetic and copies ran while one was open for 18% of the time, Pallas kernels for 0%

commit v1 on v0

--- a/solution.py
+++ b/solution.py
@@ -3,6 +3,7 @@
 import jax.numpy as jnp
 from jax import lax
 from jax.sharding import PartitionSpec as P
+from jax.lax import all_to_all, axis_size
 
 QW = 128
 QH = 64
@@ -57,13 +58,22 @@
 
 
 def shards(grad_volume, query_feats, support_feats, query_kernel, support_kernel):
+
+    def runs_get(arr):
+        mat_out = axis_size("blk")
+        last = jnp.split(arr, mat_out, 2)
+        lower = jnp.stack(last, axis=0)
+        after = all_to_all(lower, "blk", split_axis=0, concat_axis=0)
+        r2 = jnp.concatenate(after, axis=0)
+        return r2
+
     planes, columns, queries = grad_volume.shape
     rimmed = extended(grad_volume, ((("blk", "sub"), 0), ("pair", 1)), 1)
     corr_grad = (
         query_pass(grad_volume, query_kernel)
         + support_pass(rimmed, support_kernel, planes, columns)
     ).astype(jnp.bfloat16)
-    moved = lax.all_to_all(corr_grad, "blk", split_axis=2, concat_axis=0, tiled=True)
+    moved = runs_get(corr_grad)
     cycle_size = lax.axis_size("blk")
     own_index = lax.axis_index("blk")
     tile_len = moved.shape[2]

time: 320 us -> 255 us (0.80)
  other arithmetic: 70.3 us -> 26.1 us
  local copies, waits for them, and re-layouts: 28.6 us -> 6.58 us
    unnamed x3 -> x2, other arithmetic: 45.5 us -> 0.24 us
    all_to_all x2 -> x0, local copies, waits for them, and re-layouts: 8.96 us -> none  [shards(): lax.all_to_all(corr_grad, 'blk', split_axis=2, concat_axis=0, tiled=True)]
    unnamed x16 -> x10, local copies, waits for them, and re-layouts: 7.52 us -> 0.46 us
    convert_element_type x1 -> x0, local copies, waits for them, and re-layouts: 6.78 us -> none  [shards(): corr_grad = (query_pass(grad_volume, query_kernel) + support_pass(rimmed,...]
  transfers between devices with their start and end apart: 14 -> 14, of which waited for: 5 -> 5; matrix products, arithmetic and copies ran while one was open for 18% -> 22% of each run, Pallas kernels for 0% -> 0%
where the time goes in v1:
time: 255 us; the launch traced here: 254 us
  waiting for transfers between devices  145 us (57%)
  matrix products  40.3 us (16%)
  other arithmetic  26.1 us (10%)
  starting transfers between devices  21.8 us (9%)
  between operations  14.2 us (6%)
  local copies, waits for them, and re-layouts  6.58 us (3%)
    reduce_scatter x1, waiting for transfers between devices, shards(): lax.psum_scatter(query_total, ('sub', 'pair'), scatter_dimension=0, tiled...  70.9 us
    ppermute x2, waiting for transfers between devices, extended(): lax.ppermute(tail, axis, [(i, (i + 1) % count) for i in range(ends)])  40.5 us
    dot_general x4, matrix products, project(): lax.dot_general(block, feat_flat, (((0,), (0,)), ((), ())), preferred_ele...  28.2 us
    all_to_all x1, waiting for transfers between devices, runs_get(): after = all_to_all(lower, 'blk', split_axis=0, concat_axis=0)  27 us
    dot_general x4, matrix products, project(): jnp.dot(block, query_feats, preferred_element_type=jnp.float32)  12.1 us
    convert_element_type x1, other arithmetic, shards(): corr_grad = (query_pass(grad_volume, query_kernel) + support_pass(rimmed,...  11.2 us
    add x1, other arithmetic, query_pass(): total + kernel[row_shift, col_shift] * padded[:, :, row_shift:row_shift +...  9.56 us
    all_to_all x1, starting transfers between devices, runs_get(): after = all_to_all(lower, 'blk', split_axis=0, concat_axis=0)  6.94 us
  transfers between devices with their start and end apart: 14, of which 5 were waited for; matrix products, arithmetic and copies ran while one was open for 22% of the time, Pallas kernels for 0%

profile of v1, /device:TPU:0, one launch (start us, length us, event | category | flops | bytes accessed | tf_op | source)
XLA Modules:
  0.0 253.7 jit_solution(7374749532282906180)
XLA Ops:
  7.2 0.0 copy-start.3
  7.2 5.0 %collective-permute-start.2 = (bf16[1,64,8192]{2,1,0:T(8,128)(2,1)}, bf16[1,64,8192]{2,1,0:T(8,128)(2,1)S(1)}, u32[]{:S(2)}, u32[]{:S(2)}) collective-permute-start(bf16[1,64,8192]{2,1,0:T(8,128)(2,1)} %param.7), channel_id=1, source_target_pairs={{0,2},{2,4},{4,6},{6,8},{8,10},{10,12},{12,14},{1,3},{3,5},{5,7},{... | collective-permute-start | bytes 3145736 | tf_op jit(solution)/shard_map/ppermute | solution.py:20
  12.2 1.3 collective-permute-start.3
  13.5 1.7 fusion.33
  15.2 1.7 fusion.32
  16.9 40.5 %collective-permute-done.2 = bf16[1,64,8192]{2,1,0:T(8,128)(2,1)S(1)} collective-permute-done((bf16[1,64,8192]{2,1,0:T(8,128)(2,1)}, bf16[1,64,8192]{2,1,0:T(8,128)(2,1)S(1)}, u32[]{:S(2)}, u32[]{:S(2)}) %collective-permute-start.2) | collective-permute-done | bytes 1048608 | tf_op jit(solution)/shard_map/ppermute | solution.py:20
  57.3 0.1 constant_dynamic-update-slice_fusion.2
  57.4 0.2 constant_dynamic-update-slice_fusion.1
  57.7 0.0 collective-permute-done.3
  57.7 0.1 constant_dynamic-update-slice_fusion
  57.8 1.0 fusion.31
  58.8 1.3 collective-permute-start.4
  60.1 1.3 collective-permute-start.5
  61.4 0.4 copy.7
  61.8 9.6 %fusion.23 = f32[1,64,64,128]{3,2,1,0:T(8,128)S(1)} fusion(f32[1,64,64,128]{3,2,1,0:T(8,128)S(1)} %bitcast.56, f32[]{:T(128)} %bitcast.8, f32[]{:T(128)} %bitcast.7, f32[]{:T(128)} %bitcast.6, f32[]{:T(128)} %bitcast.5, f32[]{:T(128)} %bitcast.4, f32[]{:T(128)} %bitcast.3, f32[]{:T(128)} %bitcast.2, f32[]{:T(128)} %bitcast.1, f32[]{:T(128)} %bitcast), kind=kLoop, calls=%fused_computation.35 | loop fusion | flops 8912896 | bytes 4194340 | tf_op jit(solution)/shard_map/add | solution.py:43
  71.4 1.5 reshape.54
  72.9 0.0 collective-permute-done.4
  72.9 0.0 collective-permute-done.5
  72.9 11.2 %fusion.14 = bf16[1,64,8192]{2,1,0:T(8,128)(2,1)S(1)} fusion(f32[1,64,8192]{2,1,0:T(8,128)} %reshape.54, bf16[1,64,8192]{2,1,0:T(8,128)(2,1)} %param.7, bf16[1,64,8192]{2,1,0:T(8,128)(2,1)} %copy-done.2, bf16[1,64,8192]{2,1,0:T(8,128)(2,1)S(1)} %collective-permute-done.2, bf16[3,1,8192]{2,1,0:T(2,128)(2,1)S(1)} %collective-permute-done.5, ...), kind=kLoop, calls=%fused_computation.26 | loop fusion | flops 24117248 | bytes 9535524 | tf_op jit(solution)/shard_map/convert_element_type | solution.py:75
  84.1 0.1 slice_bitcast_fusion.3
  84.2 0.0 copy-start.1
  84.2 1.1 pad_maximum_fusion.2
  85.3 6.9 %all-to-all-start = ((bf16[4,1,64,2048]{3,2,1,0:T(8,128)(2,1)}), bf16[4,1,64,2048]{3,2,1,0:T(8,128)(2,1)S(1)}, u32[]{:S(2)}, u32[]{:S(2)}) async-start(bf16[4,1,64,2048]{3,2,1,0:T(8,128)(2,1)} %pad_maximum_fusion.2), calls=%async_computation | async-start | bytes 2097152 | tf_op jit(solution)/shard_map/all_to_all | solution.py:66
  92.3 27.0 %all-to-all-done = bf16[4,1,64,2048]{3,2,1,0:T(8,128)(2,1)S(1)} async-done(((bf16[4,1,64,2048]{3,2,1,0:T(8,128)(2,1)}), bf16[4,1,64,2048]{3,2,1,0:T(8,128)(2,1)S(1)}, u32[]{:S(2)}, u32[]{:S(2)}) %all-to-all-start) | async-done | bytes 1048608 | tf_op jit(solution)/shard_map/all_to_all | solution.py:66
  119.3 52.7 %while.20 = (s32[]{:T(128)}, f32[2048,1024]{1,0:T(8,128)}, bf16[1,64,1024]{2,1,0:T(8,128)(2,1)S(1)}, f32[1,64,1024]{2,1,0:T(8,128)S(1)}, s32[]{:T(128)}, /*index...) while((s32[]{:T(128)}, f32[2048,1024]{1,0:T(8,128)}, ...), condition=%wide.region_1.2_spmd.clone, body=%wide.region_0.1_spmd.clone.sunk | while | flops 541130752 | bytes 23986536 | solution.py:108
  119.4 0.1 collective-permute-start
  119.4 3.0 %fusion.44 = f32[1,64,1024]{2,1,0:T(8,128)S(1)} fusion(f32[1,64,1024]{2,1,0:T(8,128)S(1)} %get-tuple-element.303, bf16[2048,1024]{1,0:T(8,128)(2,1)} %get-tuple-element.317, bf16[4,1,64,2048]{3,2,1,0:T(8,128)(2,1)S(1)} %get-tuple-element.316, s32[]{:T(128)S(6)} %select_n.36), kind=kOutput, calls=%fused_computation.2.clone.1 | convolution fusion | flops 268500992 | bytes 4980740 | tf_op jit(solution)/shard_map/while/body/eval_jaxpr/dot_general | solution.py:91
  122.5 0.2 collective-permute-start.1
  122.7 4.5 %select_add_fusion.2 = f32[2048,1024]{1,0:T(8,128)} fusion(f32[2048,1024]{1,0:T(8,128)} %get-tuple-element.301, pred[]{:T(512)S(6)} %compare.5, bf16[4,1,64,2048]{3,2,1,0:T(8,128)(2,1)S(1)} %get-tuple-element.316, s32[]{:T(128)S(6)} %select_n.36, bf16[1,64,1024]{2,1,0:T(8,128)(2,1)S(1)} %copy.16), kind=kOutput, calls=%fused_computation.clone.1 | convolution fusion | flops 272629760 | bytes 17170436 | tf_op jit(solution)/shard_map/while/body/eval_jaxpr/dot_general | solution.py:88
  127.2 5.3 %collective-permute-done.1 = f32[1,64,1024]{2,1,0:T(8,128)S(1)} collective-permute-done((f32[1,64,1024]{2,1,0:T(8,128)S(1)}, f32[1,64,1024]{2,1,0:T(8,128)S(1)}, u32[]{:S(2)}, u32[]{:S(2)}) %collective-permute-start.1) | collective-permute-done | bytes 262176 | tf_op jit(solution)/shard_map/while/body/eval_jaxpr/ppermute | solution.py:32
  132.6 0.1 collective-permute-start
  132.6 3.0 %fusion.44 = f32[1,64,1024]{2,1,0:T(8,128)S(1)} fusion(f32[1,64,1024]{2,1,0:T(8,128)S(1)} %get-tuple-element.303, bf16[2048,1024]{1,0:T(8,128)(2,1)} %get-tuple-element.317, bf16[4,1,64,2048]{3,2,1,0:T(8,128)(2,1)S(1)} %get-tuple-element.316, s32[]{:T(128)S(6)} %select_n.36), kind=kOutput, calls=%fused_computation.2.clone.1 | convolution fusion | flops 268500992 | bytes 4980740 | tf_op jit(solution)/shard_map/while/body/eval_jaxpr/dot_general | solution.py:91
  135.7 0.5 collective-permute-start.1
  136.2 7.9 %select_add_fusion.2 = f32[2048,1024]{1,0:T(8,128)} fusion(f32[2048,1024]{1,0:T(8,128)} %get-tuple-element.301, pred[]{:T(512)S(6)} %compare.5, bf16[4,1,64,2048]{3,2,1,0:T(8,128)(2,1)S(1)} %get-tuple-element.316, s32[]{:T(128)S(6)} %select_n.36, bf16[1,64,1024]{2,1,0:T(8,128)(2,1)S(1)} %copy.16), kind=kOutput, calls=%fused_computation.clone.1 | convolution fusion | flops 272629760 | bytes 17170436 | tf_op jit(solution)/shard_map/while/body/eval_jaxpr/dot_general | solution.py:88
  144.1 0.9 collective-permute-done.1
  145.0 1.5 collective-permute-start
  146.5 3.0 %fusion.44 = f32[1,64,1024]{2,1,0:T(8,128)S(1)} fusion(f32[1,64,1024]{2,1,0:T(8,128)S(1)} %get-tuple-element.303, bf16[2048,1024]{1,0:T(8,128)(2,1)} %get-tuple-element.317, bf16[4,1,64,2048]{3,2,1,0:T(8,128)(2,1)S(1)} %get-tuple-element.316, s32[]{:T(128)S(6)} %select_n.36), kind=kOutput, calls=%fused_computation.2.clone.1 | convolution fusion | flops 268500992 | bytes 4980740 | tf_op jit(solution)/shard_map/while/body/eval_jaxpr/dot_general | solution.py:91
  149.5 2.2 collective-permute-start.1
  151.7 7.9 %select_add_fusion.2 = f32[2048,1024]{1,0:T(8,128)} fusion(f32[2048,1024]{1,0:T(8,128)} %get-tuple-element.301, pred[]{:T(512)S(6)} %compare.5, bf16[4,1,64,2048]{3,2,1,0:T(8,128)(2,1)S(1)} %get-tuple-element.316, s32[]{:T(128)S(6)} %select_n.36, bf16[1,64,1024]{2,1,0:T(8,128)(2,1)S(1)} %copy.16), kind=kOutput, calls=%fused_computation.clone.1 | convolution fusion | flops 272629760 | bytes 17170436 | tf_op jit(solution)/shard_map/while/body/eval_jaxpr/dot_general | solution.py:88
  159.6 0.1 collective-permute-start
  159.7 3.0 %fusion.44 = f32[1,64,1024]{2,1,0:T(8,128)S(1)} fusion(f32[1,64,1024]{2,1,0:T(8,128)S(1)} %get-tuple-element.303, bf16[2048,1024]{1,0:T(8,128)(2,1)} %get-tuple-element.317, bf16[4,1,64,2048]{3,2,1,0:T(8,128)(2,1)S(1)} %get-tuple-element.316, s32[]{:T(128)S(6)} %select_n.36), kind=kOutput, calls=%fused_computation.2.clone.1 | convolution fusion | flops 268500992 | bytes 4980740 | tf_op jit(solution)/shard_map/while/body/eval_jaxpr/dot_general | solution.py:91
  162.8 1.4 collective-permute-start.1
  164.2 7.9 %select_add_fusion.2 = f32[2048,1024]{1,0:T(8,128)} fusion(f32[2048,1024]{1,0:T(8,128)} %get-tuple-element.301, pred[]{:T(512)S(6)} %compare.5, bf16[4,1,64,2048]{3,2,1,0:T(8,128)(2,1)S(1)} %get-tuple-element.316, s32[]{:T(128)S(6)} %select_n.36, bf16[1,64,1024]{2,1,0:T(8,128)(2,1)S(1)} %copy.16), kind=kOutput, calls=%fused_computation.clone.1 | convolution fusion | flops 272629760 | bytes 17170436 | tf_op jit(solution)/shard_map/while/body/eval_jaxpr/dot_general | solution.py:88
  172.1 0.0 collective-permute-done.1
  172.1 0.0 reduce-scatter.2.cloned.1.call-update
  172.1 0.7 broadcast_multiply_fusion.1
  172.8 70.9 %reduce-scatter.2.cloned.1.call-done = f32[512,1024]{1,0:T(8,128)} async-done(((f32[2048,1024]{1,0:T(8,128)}), f32[512,1024]{1,0:T(8,128)}) %reduce-scatter.2.cloned.1.call-update) | async-done | bytes 2097168 | tf_op jit(solution)/shard_map/reduce_scatter | solution.py:110
  243.7 3.2 %broadcast_multiply_fusion = f32[512,1024]{1,0:T(8,128)} fusion(f32[512,1024]{1,0:T(8,128)} %reduce-scatter.2.cloned.1.call-done), kind=kLoop, calls=%fused_computation.46 | loop fusion | flops 524288 | bytes 4194304 | tf_op jit(solution)/shard_map/mul | solution.py:110
  (18 shorter events, 0.1 us)
Async XLA Ops:
  7.2 50.3 %copy-start.3 = (bf16[1,64,8192]{2,1,0:T(8,128)(2,1)S(1)}, bf16[1,64,8192]{2,1,0:T(8,128)(2,1)}, u32[]{:S(2)}) copy-start(bf16[1,64,8192]{2,1,0:T(8,128)(2,1)} %param.7) | copy-start | bytes 3145732
  7.2 50.2 %collective-permute-start.2 = (bf16[1,64,8192]{2,1,0:T(8,128)(2,1)}, bf16[1,64,8192]{2,1,0:T(8,128)(2,1)S(1)}, u32[]{:S(2)}, u32[]{:S(2)}) collective-permute-start(bf16[1,64,8192]{2,1,0:T(8,128)(2,1)} %param.7), channel_id=1, source_target_pairs={{0,2},{2,4},{4,6},{6,8},{8,10},{10,12},{12,14},{1,3},{3,5},{5,7},{... | collective-permute-start | bytes 3145736 | tf_op jit(solution)/shard_map/ppermute | solution.py:20
  12.2 45.5 %collective-permute-start.3 = (bf16[1,64,8192]{2,1,0:T(8,128)(2,1)}, bf16[1,64,8192]{2,1,0:T(8,128)(2,1)S(1)}, u32[]{:S(2)}, u32[]{:S(2)}) collective-permute-start(bf16[1,64,8192]{2,1,0:T(8,128)(2,1)} %param.7), channel_id=1, source_target_pairs={{2,0},{4,2},{6,4},{8,6},{10,8},{12,10},{14,12},{3,1},{5,3},{7,5},{... | collective-permute-start | bytes 3145736 | tf_op jit(solution)/shard_map/ppermute | solution.py:22
  57.7 4.1 %copy-start.2 = (bf16[1,64,8192]{2,1,0:T(8,128)(2,1)}, bf16[1,64,8192]{2,1,0:T(8,128)(2,1)S(1)}, u32[]{:S(2)}) copy-start(bf16[1,64,8192]{2,1,0:T(8,128)(2,1)S(1)} %collective-permute-done.3) | copy-start | bytes 3145732
  57.8 4.0 %copy-start = (bf16[3,64,8192]{2,1,0:T(8,128)(2,1)}, bf16[3,64,8192]{2,1,0:T(8,128)(2,1)S(1)}, u32[]{:S(2)}) copy-start(bf16[3,64,8192]{2,1,0:T(8,128)(2,1)S(1)} %constant_dynamic-update-slice_fusion) | copy-start | bytes 9437188
  58.8 14.1 %collective-permute-start.4 = (bf16[3,1,8192]{2,1,0:T(2,128)(2,1)}, bf16[3,1,8192]{2,1,0:T(2,128)(2,1)S(1)}, u32[]{:S(2)}, u32[]{:S(2)}) collective-permute-start(bf16[3,1,8192]{2,1,0:T(2,128)(2,1)} %get-tuple-element.220), channel_id=1, source_target_pairs={{0,1},{2,3},{4,5},{6,7},{8,9},{10,11},{12,13},{14,15},{16,17},{18,... | collective-permute-start | bytes 147464 | tf_op jit(solution)/shard_map/ppermute | solution.py:20
  60.1 12.8 %collective-permute-start.5 = (bf16[3,1,8192]{2,1,0:T(2,128)(2,1)S(1)}, bf16[3,1,8192]{2,1,0:T(2,128)(2,1)S(1)}, u32[]{:S(2)}, u32[]{:S(2)}) collective-permute-start(bf16[3,1,8192]{2,1,0:T(2,128)(2,1)S(1)} %get-tuple-element.221), channel_id=1, source_target_pairs={{1,0},{3,2},{5,4},{7,6},{9,8},{11,10},{13,12},{15,14},{17,16},{19,... | collective-permute-start | bytes 147464 | tf_op jit(solution)/shard_map/ppermute | solution.py:22
  84.2 35.1 %copy-start.1 = (bf16[1,64,1024]{2,1,0:T(8,128)(2,1)S(1)}, bf16[1,64,1024]{2,1,0:T(8,128)(2,1)}, u32[]{:S(2)}) copy-start(bf16[1,64,1024]{2,1,0:T(8,128)(2,1)} %param.9) | copy-start | bytes 393220
  85.3 34.0 %all-to-all-start = ((bf16[4,1,64,2048]{3,2,1,0:T(8,128)(2,1)}), bf16[4,1,64,2048]{3,2,1,0:T(8,128)(2,1)S(1)}, u32[]{:S(2)}, u32[]{:S(2)}) async-start(bf16[4,1,64,2048]{3,2,1,0:T(8,128)(2,1)} %pad_maximum_fusion.2), calls=%async_computation | async-start | bytes 2097152 | tf_op jit(solution)/shard_map/all_to_all | solution.py:66
  92.3 151.4 %reduce-scatter.2.cloned.1.call-start = ((), (), s32[]{:S(2)}) async-start(), calls=%async_computation.2 | async-start | bytes 10485760 | tf_op jit(solution)/shard_map/reduce_scatter | solution.py:110
  119.4 7.9 %collective-permute-start = (bf16[1,64,1024]{2,1,0:T(8,128)(2,1)S(1)}, bf16[1,64,1024]{2,1,0:T(8,128)(2,1)S(1)}, u32[]{:S(2)}, u32[]{:S(2)}) collective-permute-start(bf16[1,64,1024]{2,1,0:T(8,128)(2,1)S(1)} %copy.16), channel_id=1, source_target_pairs={{0,4},{4,8},{8,12},{12,0},{1,5},{5,9},{9,13},{13,1},{2,6},{6,10},{... | collective-permute-start | bytes 393224 | tf_op jit(solution)/shard_map/while/body/eval_jaxpr/ppermute | solution.py:32
  122.5 10.1 %collective-permute-start.1 = (f32[1,64,1024]{2,1,0:T(8,128)S(1)}, f32[1,64,1024]{2,1,0:T(8,128)S(1)}, u32[]{:S(2)}, u32[]{:S(2)}) collective-permute-start(f32[1,64,1024]{2,1,0:T(8,128)S(1)} %fusion.44), channel_id=1, source_target_pairs={{0,4},{4,8},{8,12},{12,0},{1,5},{5,9},{9,13},{13,1},{2,6},{6,10},{... | collective-permute-start | bytes 786440 | tf_op jit(solution)/shard_map/while/body/eval_jaxpr/ppermute | solution.py:32
  132.6 11.5 %collective-permute-start = (bf16[1,64,1024]{2,1,0:T(8,128)(2,1)S(1)}, bf16[1,64,1024]{2,1,0:T(8,128)(2,1)S(1)}, u32[]{:S(2)}, u32[]{:S(2)}) collective-permute-start(bf16[1,64,1024]{2,1,0:T(8,128)(2,1)S(1)} %copy.16), channel_id=1, source_target_pairs={{0,4},{4,8},{8,12},{12,0},{1,5},{5,9},{9,13},{13,1},{2,6},{6,10},{... | collective-permute-start | bytes 393224 | tf_op jit(solution)/shard_map/while/body/eval_jaxpr/ppermute | solution.py:32
  135.7 9.3 %collective-permute-start.1 = (f32[1,64,1024]{2,1,0:T(8,128)S(1)}, f32[1,64,1024]{2,1,0:T(8,128)S(1)}, u32[]{:S(2)}, u32[]{:S(2)}) collective-permute-start(f32[1,64,1024]{2,1,0:T(8,128)S(1)} %fusion.44), channel_id=1, source_target_pairs={{0,4},{4,8},{8,12},{12,0},{1,5},{5,9},{9,13},{13,1},{2,6},{6,10},{... | collective-permute-start | bytes 786440 | tf_op jit(solution)/shard_map/while/body/eval_jaxpr/ppermute | solution.py:32
  145.0 14.6 %collective-permute-start = (bf16[1,64,1024]{2,1,0:T(8,128)(2,1)S(1)}, bf16[1,64,1024]{2,1,0:T(8,128)(2,1)S(1)}, u32[]{:S(2)}, u32[]{:S(2)}) collective-permute-start(bf16[1,64,1024]{2,1,0:T(8,128)(2,1)S(1)} %copy.16), channel_id=1, source_target_pairs={{0,4},{4,8},{8,12},{12,0},{1,5},{5,9},{9,13},{13,1},{2,6},{6,10},{... | collective-permute-start | bytes 393224 | tf_op jit(solution)/shard_map/while/body/eval_jaxpr/ppermute | solution.py:32
  149.5 10.1 %collective-permute-start.1 = (f32[1,64,1024]{2,1,0:T(8,128)S(1)}, f32[1,64,1024]{2,1,0:T(8,128)S(1)}, u32[]{:S(2)}, u32[]{:S(2)}) collective-permute-start(f32[1,64,1024]{2,1,0:T(8,128)S(1)} %fusion.44), channel_id=1, source_target_pairs={{0,4},{4,8},{8,12},{12,0},{1,5},{5,9},{9,13},{13,1},{2,6},{6,10},{... | collective-permute-start | bytes 786440 | tf_op jit(solution)/shard_map/while/body/eval_jaxpr/ppermute | solution.py:32
  159.6 12.4 %collective-permute-start = (bf16[1,64,1024]{2,1,0:T(8,128)(2,1)S(1)}, bf16[1,64,1024]{2,1,0:T(8,128)(2,1)S(1)}, u32[]{:S(2)}, u32[]{:S(2)}) collective-permute-start(bf16[1,64,1024]{2,1,0:T(8,128)(2,1)S(1)} %copy.16), channel_id=1, source_target_pairs={{0,4},{4,8},{8,12},{12,0},{1,5},{5,9},{9,13},{13,1},{2,6},{6,10},{... | collective-permute-start | bytes 393224 | tf_op jit(solution)/shard_map/while/body/eval_jaxpr/ppermute | solution.py:32
  162.8 9.3 %collective-permute-start.1 = (f32[1,64,1024]{2,1,0:T(8,128)S(1)}, f32[1,64,1024]{2,1,0:T(8,128)S(1)}, u32[]{:S(2)}, u32[]{:S(2)}) collective-permute-start(f32[1,64,1024]{2,1,0:T(8,128)S(1)} %fusion.44), channel_id=1, source_target_pairs={{0,4},{4,8},{8,12},{12,0},{1,5},{5,9},{9,13},{13,1},{2,6},{6,10},{... | collective-permute-start | bytes 786440 | tf_op jit(solution)/shard_map/while/body/eval_jaxpr/ppermute | solution.py:32
Sparse Core Ops, SparseCore 0:
  172.2 71.4 reduce-scatter.1
